TPU v7x, 256 devices: a whole 4x4x8 slice. The times are simulated.
256 devices in a mesh: az: 128 (over z, y, x_hi, core), rd: 2 (over x_lo).
Axes of the slice: x: 4 (x_hi: 2, x_lo: 2; x = x_hi * 2 + x_lo), y: 4, z: 8, core: 2. Of those that a mesh axis runs over, the one named last changes fastest.
Arguments:
- echoes: bfloat16 [2, 2048, 32, 2048], P(None, 'az', None, 'rd'), may hold values from -6 to 6
- pulse_taper: float32 [32], replicated, may hold values from 0.1 to 1.9
- beam_weights: float32 [5], replicated, may hold values from 0.3 to 1
- blanking: int32 [2048, 16], P('az'), may hold values 0 or 1
- cfar_sizes: int32 [6], replicated, may hold values from 1 to 23, as said below
Outputs:
- detection: bfloat16 [2048, 32, 2048], P('az', 'rd')
Inputs may be any that keep to these rules, and one draw needn't show every extreme that they name: `cfar_sizes`: the range guard (entry 0) is 1; the Doppler and azimuth guards (entries 2, 4) are 1 or 2; guard plus window is exactly 24 for range (entries 0, 1), 4 for Doppler (2, 3) and 12 for azimuth (4, 5).
All inputs are finite; a program needn't handle non-finite values. No bound on the sum of `blanking` on one device may be relied on, other than what follows from the above.
Results may differ from a plain program's by a relative error of at most 0.012.
Values may be sent and summed in bfloat16 or wider, within the bound.
A program may use at most 64 MiB of HBM per device.

v0:
```python
import math
import jax
import jax.numpy as jnp
from jax import lax
from jax.sharding import PartitionSpec as P

REACH_R = 24
REACH_D = 4
REACH_A = 12
BLANK_CELLS = 128


def with_halo(cells, sides, width, closed):
    for axis, dim in sides:
        count = lax.axis_size(axis)
        ends = count if closed else count - 1
        head = lax.slice_in_dim(cells, 0, width, axis=dim)
        tail = lax.slice_in_dim(cells, cells.shape[dim] - width, cells.shape[dim], axis=dim)
        cells = jnp.concatenate(
            [
                lax.ppermute(tail, axis, [(i, (i + 1) % count) for i in range(ends)]),
                cells,
                lax.ppermute(head, axis, [((i + 1) % count, i) for i in range(ends)]),
            ],
            axis=dim,
        )
    return cells


def bank_matrix(pulse_taper):
    pulses = pulse_taper.shape[0]
    indices = jnp.arange(pulses, dtype=jnp.int32)
    phases = indices[:, None] * indices[None, :] % pulses
    angles = phases.astype(jnp.float32) * (2.0 * math.pi / pulses)
    cosines = jnp.cos(angles) * pulse_taper[None, :]
    sine_terms = jnp.sin(angles) * pulse_taper[None, :]
    real_row = jnp.stack([cosines, sine_terms], axis=1)
    imag_row = jnp.stack([-sine_terms, cosines], axis=1)
    return jnp.stack([real_row, imag_row], axis=0).astype(jnp.bfloat16)


def window_bands(extended, length, reach, guard):
    rows_index = lax.broadcasted_iota(jnp.int32, (extended, length), 0)
    cols_index = lax.broadcasted_iota(jnp.int32, (extended, length), 1)
    before = cols_index + reach - rows_index
    after = rows_index - cols_index - reach
    leading = ((before > guard) & (before <= reach)).astype(jnp.bfloat16)
    lagging = ((after > guard) & (after <= reach)).astype(jnp.bfloat16)
    return (leading, lagging)


def local(echoes, pulse_taper, beam_weights, blanking, cfar_sizes):
    pulses = pulse_taper.shape[0]
    dwells = echoes.shape[1]
    bank = bank_matrix(pulse_taper)
    spectrum = jnp.einsum("ckdp,dapr->cakr", bank, echoes, preferred_element_type=jnp.float32)
    powers = (spectrum[0] * spectrum[0] + spectrum[1] * spectrum[1]) / pulses
    margin = 0
    beside_all = with_halo(powers, (("az", 0),), 2, True)
    span = dwells + 2 * margin
    integrated = beam_weights[0] * beside_all[0:span]
    for offset in range(1, 5):
        integrated = integrated + beam_weights[offset] * beside_all[offset : offset + span]
    log_power = jnp.log(integrated + 0.05).astype(jnp.bfloat16)
    log_power = with_halo(log_power, (("az", 0),), REACH_A, True)
    center = log_power[REACH_A : REACH_A + dwells]
    local_bins = center.shape[1]
    local_cells = center.shape[2]
    guard_range = cfar_sizes[0]
    guard_doppler = cfar_sizes[2]
    window_doppler = cfar_sizes[3].astype(jnp.float32)
    guard_azimuth = cfar_sizes[4]
    window_azimuth = cfar_sizes[5].astype(jnp.float32)
    lead_band, lag_band = window_bands(dwells + 2 * REACH_A, dwells, REACH_A, guard_azimuth)
    azimuth_lead = (
        jnp.einsum("sb,sqr->bqr", lead_band, log_power, preferred_element_type=jnp.float32)
        / window_azimuth
    )
    azimuth_lag = (
        jnp.einsum("sb,sqr->bqr", lag_band, log_power, preferred_element_type=jnp.float32)
        / window_azimuth
    )
    offset_cells = lax.axis_index("rd") * local_cells
    total_cells = local_cells * lax.axis_size("rd")
    widened = with_halo(center, (("rd", 2),), REACH_R, False)
    positions = offset_cells - REACH_R + jnp.arange(local_cells + 2 * REACH_R, dtype=jnp.int32)
    inside = ((positions >= 0) & (positions < total_cells)).astype(jnp.float32)
    block_count = blanking.shape[1]
    block_ids = jnp.clip(positions // BLANK_CELLS, 0, block_count - 1)
    selector = (block_ids[None, :] == jnp.arange(block_count, dtype=jnp.int32)[:, None]).astype(
        jnp.float32
    )
    weight = (
        jnp.dot(blanking.astype(jnp.float32), selector, precision=lax.Precision.HIGHEST)
        * inside[None, :]
    )
    weighted = widened * weight[:, None, :].astype(jnp.bfloat16)
    pieces = local_cells // BLANK_CELLS
    extent = BLANK_CELLS + 2 * REACH_R
    value_blocks = jnp.stack(
        [
            weighted[:, :, number * BLANK_CELLS : number * BLANK_CELLS + extent]
            for number in range(pieces)
        ],
        axis=2,
    )
    weight_blocks = jnp.stack(
        [
            weight[:, number * BLANK_CELLS : number * BLANK_CELLS + extent]
            for number in range(pieces)
        ],
        axis=1,
    )
    range_lead_band, range_lag_band = window_bands(extent, BLANK_CELLS, REACH_R, guard_range)

    def range_mean(banded):
        sums = jnp.einsum("aqbs,sr->aqbr", value_blocks, banded, preferred_element_type=jnp.float32)
        sums = sums.reshape(dwells, local_bins, local_cells)
        counts = jnp.einsum(
            "abs,sr->abr",
            weight_blocks,
            banded.astype(jnp.float32),
            precision=lax.Precision.HIGHEST,
        )
        counts = counts.reshape(dwells, local_cells)
        return sums / jnp.maximum(counts, 1.0)[:, None, :]

    range_lead = range_mean(range_lead_band)
    range_lag = range_mean(range_lag_band)
    circled = jnp.concatenate(
        [center[:, local_bins - REACH_D :], center, center[:, :REACH_D]], axis=1
    )
    doppler_lead_band, doppler_lag_band = window_bands(
        local_bins + 2 * REACH_D, local_bins, REACH_D, guard_doppler
    )
    doppler_lead = (
        jnp.einsum("asr,sk->akr", circled, doppler_lead_band, preferred_element_type=jnp.float32)
        / window_doppler
    )
    doppler_lag = (
        jnp.einsum("asr,sk->akr", circled, doppler_lag_band, preferred_element_type=jnp.float32)
        / window_doppler
    )
    noise_level = jnp.maximum(
        jnp.maximum(range_lead, range_lag), jnp.maximum(doppler_lead, doppler_lag)
    )
    noise_level = jnp.maximum(noise_level, jnp.maximum(azimuth_lead, azimuth_lag))
    keep = weight[:, REACH_R : REACH_R + local_cells]
    detection = (keep[:, None, :] * (center.astype(jnp.float32) - noise_level)).astype(jnp.bfloat16)
    detection = lax.all_to_all(detection, "rd", split_axis=1, concat_axis=2, tiled=True)
    return detection


def solution(mesh):
    in_specs = (P(None, "az", None, "rd"), P(), P(), P("az", None), P())
    out_specs = P("az", "rd", None)
    return jax.shard_map(local, mesh=mesh, in_specs=in_specs, out_specs=out_specs, check_vma=False)
```

profile of v0, /device:TPU:1, one launch (start us, length us, event | category | flops | bytes accessed | tf_op | source)
XLA Modules:
  0.0 95.5 jit_solution(6288917200939661095)
XLA Ops:
  0.0 0.7 fusion.75
  0.8 2.3 %convolution_bitcast_fusion = f32[2,16,32,1024]{3,2,1,0:T(8,128)S(1)} fusion(bf16[2,16,32,1024]{3,2,1,0:T(8,128)(2,1)} %param.5, bf16[1,32,2,32]{3,1,2,0:T(8,128)(2,1)S(1)} %get-tuple-element.14, bf16[1,32,2,32]{3,1,2,0:T(8,128)(2,1)S(1)} %get-tuple-element.13), kind=kOutput, calls=%fused_computation.11 | convolution fusion | flops 134234112 | bytes 6299648 | tf_op jit(solution)/shard_map/ckdp,dapr->cakr/dot_general | solution.py:56
  3.1 0.0 copy-start
  3.1 0.7 broadcast_multiply_fusion
  3.8 3.3 %collective-permute-start.1 = (f32[2,32,1024]{2,1,0:T(8,128)S(1)}, f32[2,32,1024]{2,1,0:T(8,128)S(1)}, u32[]{:S(2)}, u32[]{:S(2)}) collective-permute-start(f32[2,32,1024]{2,1,0:T(8,128)S(1)} %get-tuple-element.6), channel_id=1, source_target_pairs={{2,0},{4,2},{6,4},{8,6},{10,8},{12,10},{14,12},{16,14},{18,16},{20... | collective-permute-start | bytes 786440 | tf_op jit(solution)/shard_map/ppermute | solution.py:23
  7.1 0.0 copy-start.6
  7.1 0.0 copy-start.7
  7.1 0.0 copy-start.8
  7.1 1.0 %collective-permute-start = (f32[2,32,1024]{2,1,0:T(8,128)S(1)}, f32[2,32,1024]{2,1,0:T(8,128)S(1)}, u32[]{:S(2)}, u32[]{:S(2)}) collective-permute-start(f32[2,32,1024]{2,1,0:T(8,128)S(1)} %get-tuple-element.5), channel_id=1, source_target_pairs={{0,2},{2,4},{4,6},{6,8},{8,10},{10,12},{12,14},{14,16},{16,18},{18... | collective-permute-start | bytes 786440 | tf_op jit(solution)/shard_map/ppermute | solution.py:21
  8.1 0.0 copy-done
  8.2 0.5 fusion.129
  8.7 0.0 copy-done.6
  8.7 0.7 fusion.127
  9.3 0.0 copy-done.7
  9.3 0.6 fusion.126
  10.0 0.0 copy-done.8
  10.0 0.2 fusion.128
  10.2 0.9 convolution_maximum_fusion
  11.1 0.9 convolution_maximum_fusion.1
  12.0 0.1 slice.178
  14.0 0.7 copy_bitcast_fusion
  14.6 0.0 collective-permute-done.1
  14.7 2.0 %collective-permute-done = f32[2,32,1024]{2,1,0:T(8,128)S(1)} collective-permute-done((f32[2,32,1024]{2,1,0:T(8,128)S(1)}, f32[2,32,1024]{2,1,0:T(8,128)S(1)}, u32[]{:S(2)}, u32[]{:S(2)}) %collective-permute-start) | collective-permute-done | bytes 262176 | tf_op jit(solution)/shard_map/ppermute | solution.py:21
  16.6 0.0 copy-start.3
  16.6 0.7 copy-done.3
  17.3 5.8 %fusion.11 = bf16[16,32,1024]{2,1,0:T(8,128)(2,1)S(1)} fusion(f32[16,32,1024]{2,1,0:T(8,128)S(1)} %fusion.129, f32[2,32,1024]{2,1,0:T(8,128)S(1)} %collective-permute-done.1, f32[2,32,1024]{2,1,0:T(8,128)} %copy-done.3, f32[]{:T(128)} %bitcast.18, f32[]{:T(128)} %bitcast.16, f32[]{:T(128)} %bitcast.14, f32[]{:T(128)} %bitcast.13, f32[]{:T(128)} %bitcast.1, ...), kind=kLoop, calls=%fused_computation.18 | loop fusion | flops 9437184 | bytes 7864340 | tf_op jit(solution)/shard_map/convert_element_type | solution.py:64
  23.2 1.3 %fusion.125 = (bf16[12,32,1024]{2,1,0:T(8,128)(2,1)}, bf16[12,32,1024]{2,1,0:T(8,128)(2,1)}) fusion(bf16[16,32,1024]{2,1,0:T(8,128)(2,1)S(1)} %fusion.11), kind=kLoop, calls=%fused_computation.187 | loop fusion | bytes 3145728 | tf_op jit(solution)/shard_map/slice | solution.py:18
  24.5 0.1 fusion.124
  24.6 0.1 fusion.123
  24.7 10.6 %collective-permute-start.5 = (bf16[12,32,1024]{2,1,0:T(8,128)(2,1)}, bf16[12,32,1024]{2,1,0:T(8,128)(2,1)}, u32[]{:S(2)}, u32[]{:S(2)}) collective-permute-start(bf16[12,32,1024]{2,1,0:T(8,128)(2,1)} %get-tuple-element.12), channel_id=1, source_target_pairs={{2,0},{4,2},{6,4},{8,6},{10,8},{12,10},{14,12},{16,14},{18,16},{20... | collective-permute-start | bytes 2359304 | tf_op jit(solution)/shard_map/ppermute | solution.py:23
  35.3 0.0 collective-permute-start.4
  35.3 2.2 %collective-permute-start.2 = (bf16[16,32,24]{2,1,0:T(8,128)(2,1)S(1)}, bf16[16,32,24]{2,1,0:T(8,128)(2,1)S(1)}, u32[]{:S(2)}, u32[]{:S(2)}) collective-permute-start(bf16[16,32,24]{2,1,0:T(8,128)(2,1)S(1)} %get-tuple-element.8), channel_id=1, source_target_pairs={{0,1},{2,3},{4,5},{6,7},{8,9},{10,11},{12,13},{14,15},{16,17},{18,... | collective-permute-start | bytes 73736 | tf_op jit(solution)/shard_map/ppermute | solution.py:21
  37.5 1.5 %collective-permute-start.3 = (bf16[16,32,24]{2,1,0:T(8,128)(2,1)S(1)}, bf16[16,32,24]{2,1,0:T(8,128)(2,1)S(1)}, u32[]{:S(2)}, u32[]{:S(2)}) collective-permute-start(bf16[16,32,24]{2,1,0:T(8,128)(2,1)S(1)} %get-tuple-element.7), channel_id=1, source_target_pairs={{1,0},{3,2},{5,4},{7,6},{9,8},{11,10},{13,12},{15,14},{17,16},{19,... | collective-permute-start | bytes 73736 | tf_op jit(solution)/shard_map/ppermute | solution.py:23
  39.0 2.6 %fusion.30 = f32[32,16,1024]{2,0,1:T(8,128)} fusion(bf16[16,4,1024]{2,1,0:T(4,128)(2,1)S(1)} %get-tuple-element.10, bf16[16,32,1024]{2,1,0:T(8,128)(2,1)S(1)} %fusion.11, bf16[16,4,1024]{2,1,0:T(4,128)(2,1)S(1)} %get-tuple-element.9, s32[]{:T(128)} %bitcast.42, s32[32]{0:T(128)S(1)} %iota_add_fusion.2), kind=kOutput, calls=%fused_computation.47 | convolution fusion | flops 45880320 | bytes 3408004 | tf_op jit(solution)/shard_map/asr,sk->akr/dot_general | solution.py:137
  41.6 11.1 %collective-permute-done.2 = bf16[16,32,24]{2,1,0:T(8,128)(2,1)S(1)} collective-permute-done((bf16[16,32,24]{2,1,0:T(8,128)(2,1)S(1)}, bf16[16,32,24]{2,1,0:T(8,128)(2,1)S(1)}, u32[]{:S(2)}, u32[]{:S(2)}) %collective-permute-start.2) | collective-permute-done | bytes 24608 | tf_op jit(solution)/shard_map/ppermute | solution.py:21
  52.7 1.1 %collective-permute-done.3 = bf16[16,32,24]{2,1,0:T(8,128)(2,1)S(1)} collective-permute-done((bf16[16,32,24]{2,1,0:T(8,128)(2,1)S(1)}, bf16[16,32,24]{2,1,0:T(8,128)(2,1)S(1)}, u32[]{:S(2)}, u32[]{:S(2)}) %collective-permute-start.3) | collective-permute-done | bytes 24608 | tf_op jit(solution)/shard_map/ppermute | solution.py:23
  53.9 1.9 %concatenate.20 = bf16[16,32,1072]{2,1,0:T(8,128)(2,1)S(1)} concatenate(bf16[16,32,24]{2,1,0:T(8,128)(2,1)S(1)} %collective-permute-done.2, bf16[16,32,1024]{2,1,0:T(8,128)(2,1)S(1)} %fusion.11, bf16[16,32,24]{2,1,0:T(8,128)(2,1)S(1)} %collective-permute-done.3), dimensions={2} | concatenate | bytes 2195456 | tf_op jit(solution)/shard_map/concatenate | solution.py:19
  55.8 0.1 broadcast_multiply_fusion.1
  56.1 3.3 %fusion.26 = f32[16,32,8,128]{3,2,1,0:T(8,128)} fusion(bf16[16,32,8,176]{3,1,0,2:T(8,128)(2,1)S(1)} %fusion.31, s32[]{:T(128)} %bitcast.27), kind=kOutput, calls=%fused_computation.40 | convolution fusion | flops 184662016 | bytes 3538948 | tf_op jit(solution)/shard_map/aqbs,sr->aqbr/dot_general | solution.py:117
  59.4 2.7 %reshape.196 = f32[16,32,1024]{2,1,0:T(8,128)} reshape(f32[16,32,8,128]{3,2,1,0:T(8,128)} %fusion.26) | data formatting | bytes 4194304 | tf_op jit(solution)/shard_map/reshape | solution.py:118
  62.1 3.3 %fusion.28 = f32[16,32,8,128]{3,2,1,0:T(8,128)} fusion(bf16[16,32,8,176]{3,1,0,2:T(8,128)(2,1)S(1)} %fusion.31, s32[]{:T(128)} %bitcast.27, s32[128]{0:T(128)S(1)} %iota_add_fusion.3), kind=kOutput, calls=%fused_computation.42 | convolution fusion | flops 184639488 | bytes 3539460 | tf_op jit(solution)/shard_map/aqbs,sr->aqbr/dot_general | solution.py:117
  65.4 1.7 %reshape.195 = f32[16,32,1024]{2,1,0:T(8,128)S(1)} reshape(f32[16,32,8,128]{3,2,1,0:T(8,128)} %fusion.28) | data formatting | bytes 4194304 | tf_op jit(solution)/shard_map/reshape | solution.py:118
  67.2 0.0 collective-permute-done.5
  67.2 0.0 collective-permute-done.4
  67.2 1.7 %pad_maximum_fusion = bf16[40,32,1024]{2,1,0:T(8,128)(2,1)S(1)} fusion(bf16[12,32,1024]{2,1,0:T(8,128)(2,1)} %collective-permute-done.5, bf16[16,32,1024]{2,1,0:T(8,128)(2,1)S(1)} %fusion.11, bf16[12,32,1024]{2,1,0:T(8,128)(2,1)} %collective-permute-done.4), kind=kLoop, calls=%fused_computation | loop fusion | flops 2621440 | bytes 5242880 | tf_op jit(solution)/shard_map/concatenate | solution.py:19
  68.8 3.7 %fusion = f32[16,32,1024]{2,0,1:T(8,128)S(1)} fusion(bf16[40,32,1024]{2,1,0:T(8,128)(2,1)S(1)} %pad_maximum_fusion, s32[]{:T(128)} %bitcast.47), kind=kOutput, calls=%fused_computation.5 | convolution fusion | flops 41946240 | bytes 4718596 | tf_op jit(solution)/shard_map/sb,sqr->bqr/dot_general | solution.py:80
  72.6 0.0 copy-start.1
  72.6 0.0 copy-start.2
  72.6 0.0 copy-start.4
  72.6 0.0 copy-start.5
  72.6 3.9 %fusion.2 = f32[16,32,1024]{2,0,1:T(8,128)S(1)} fusion(bf16[40,32,1024]{2,1,0:T(8,128)(2,1)S(1)} %pad_maximum_fusion, s32[]{:T(128)} %bitcast.47, s32[16]{0:T(128)S(1)} %iota_add_fusion.1), kind=kOutput, calls=%fused_computation.7 | convolution fusion | flops 41945600 | bytes 4718660 | tf_op jit(solution)/shard_map/sb,sqr->bqr/dot_general | solution.py:76
  76.5 0.0 copy-done.1
  76.5 0.0 copy-done.2
  76.5 0.0 copy-done.4
  76.5 0.0 copy-done.5
  76.5 4.2 %fusion.22 = bf16[16,32,1024]{2,1,0:T(8,128)(2,1)S(1)} fusion(f32[16,32,1024]{2,0,1:T(8,128)S(1)} %fusion, f32[16,32,1024]{2,0,1:T(8,128)S(1)} %fusion.2, f32[32,16,1024]{2,0,1:T(8,128)S(1)} %copy-done.1, f32[16,32,1024]{2,1,0:T(8,128)S(1)} %copy-done.2, f32[16,32,1024]{2,1,0:T(8,128)S(1)} %reshape.195, bf16[16,32,1024]{2,1,0:T(8,128)(2,1)S(1)} %fusion.11, ...), kind=kOutput, calls=%fused_computation.34 | convolution fusion | flops 53745920 | bytes 13041676 | tf_op jit(solution)/shard_map/asr,sk->akr/dot_general | solution.py:141
  80.8 0.6 copy.25
  81.4 11.4 %all_to_all.18 = bf16[16,32,1024]{2,0,1:T(8,128)(2,1)S(1)} all-to-all(bf16[16,32,1024]{2,0,1:T(8,128)(2,1)S(1)} %copy.25), channel_id=1, replica_groups=mesh['az'=128,'rd'=2] {'rd'}, dimensions={1} | all-to-all | bytes 2097152 | tf_op jit(solution)/shard_map/all_to_all | solution.py:150
  92.8 1.1 %copy.26 = bf16[16,16,2,1024]{3,2,1,0:T(2,128)(2,1)S(1)} copy(bf16[16,16,2,1024]{3,0,1,2:T(8,128)(2,1)S(1)} %bitcast.152) | data formatting | bytes 2097152 | tf_op jit(solution)/shard_map/all_to_all | solution.py:150
  93.9 1.6 %all_to_all.16 = bf16[16,16,2048]{2,1,0:T(8,128)(2,1)} reshape(bf16[16,16,2,1024]{3,2,1,0:T(2,128)(2,1)S(1)} %copy.26) | data formatting | bytes 2097152 | tf_op jit(solution)/shard_map/all_to_all | solution.py:150
  (23 shorter events, 0.3 us)
Async XLA Ops:
  3.1 5.0 %copy-start = (f32[2,16,32,1024]{3,2,1,0:T(8,128)}, f32[2,16,32,1024]{3,2,1,0:T(8,128)S(1)}, u32[]{:S(2)}) copy-start(f32[2,16,32,1024]{3,2,1,0:T(8,128)S(1)} %convolution_bitcast_fusion) | copy-start | bytes 12582916
  3.8 10.8 %collective-permute-start.1 = (f32[2,32,1024]{2,1,0:T(8,128)S(1)}, f32[2,32,1024]{2,1,0:T(8,128)S(1)}, u32[]{:S(2)}, u32[]{:S(2)}) collective-permute-start(f32[2,32,1024]{2,1,0:T(8,128)S(1)} %get-tuple-element.6), channel_id=1, source_target_pairs={{2,0},{4,2},{6,4},{8,6},{10,8},{12,10},{14,12},{16,14},{18,16},{20... | collective-permute-start | bytes 786440 | tf_op jit(solution)/shard_map/ppermute | solution.py:23
  7.1 1.6 %copy-start.6 = (f32[5]{0:T(128)S(1)}, f32[5]{0:T(128)}, u32[]{:S(2)}) copy-start(f32[5]{0:T(128)} %param.7) | copy-start | bytes 64
  7.1 2.2 %copy-start.7 = (s32[6]{0:T(128)S(1)}, s32[6]{0:T(128)}, u32[]{:S(2)}) copy-start(s32[6]{0:T(128)} %param.9) | copy-start | bytes 76
  7.1 2.8 %copy-start.8 = (s32[16,16]{1,0:T(8,128)S(1)}, s32[16,16]{1,0:T(8,128)}, u32[]{:S(2)}) copy-start(s32[16,16]{1,0:T(8,128)} %param.8) | copy-start | bytes 3076
  7.1 9.5 %collective-permute-start = (f32[2,32,1024]{2,1,0:T(8,128)S(1)}, f32[2,32,1024]{2,1,0:T(8,128)S(1)}, u32[]{:S(2)}, u32[]{:S(2)}) collective-permute-start(f32[2,32,1024]{2,1,0:T(8,128)S(1)} %get-tuple-element.5), channel_id=1, source_target_pairs={{0,2},{2,4},{4,6},{6,8},{8,10},{10,12},{12,14},{14,16},{16,18},{18... | collective-permute-start | bytes 786440 | tf_op jit(solution)/shard_map/ppermute | solution.py:21
  16.6 0.7 copy-start.3
  24.7 42.4 %collective-permute-start.5 = (bf16[12,32,1024]{2,1,0:T(8,128)(2,1)}, bf16[12,32,1024]{2,1,0:T(8,128)(2,1)}, u32[]{:S(2)}, u32[]{:S(2)}) collective-permute-start(bf16[12,32,1024]{2,1,0:T(8,128)(2,1)} %get-tuple-element.12), channel_id=1, source_target_pairs={{2,0},{4,2},{6,4},{8,6},{10,8},{12,10},{14,12},{16,14},{18,16},{20... | collective-permute-start | bytes 2359304 | tf_op jit(solution)/shard_map/ppermute | solution.py:23
  35.3 31.9 %collective-permute-start.4 = (bf16[12,32,1024]{2,1,0:T(8,128)(2,1)}, bf16[12,32,1024]{2,1,0:T(8,128)(2,1)}, u32[]{:S(2)}, u32[]{:S(2)}) collective-permute-start(bf16[12,32,1024]{2,1,0:T(8,128)(2,1)} %get-tuple-element.11), channel_id=1, source_target_pairs={{0,2},{2,4},{4,6},{6,8},{8,10},{10,12},{12,14},{14,16},{16,18},{18... | collective-permute-start | bytes 2359304 | tf_op jit(solution)/shard_map/ppermute | solution.py:21
  35.3 17.4 %collective-permute-start.2 = (bf16[16,32,24]{2,1,0:T(8,128)(2,1)S(1)}, bf16[16,32,24]{2,1,0:T(8,128)(2,1)S(1)}, u32[]{:S(2)}, u32[]{:S(2)}) collective-permute-start(bf16[16,32,24]{2,1,0:T(8,128)(2,1)S(1)} %get-tuple-element.8), channel_id=1, source_target_pairs={{0,1},{2,3},{4,5},{6,7},{8,9},{10,11},{12,13},{14,15},{16,17},{18,... | collective-permute-start | bytes 73736 | tf_op jit(solution)/shard_map/ppermute | solution.py:21
  37.5 16.3 %collective-permute-start.3 = (bf16[16,32,24]{2,1,0:T(8,128)(2,1)S(1)}, bf16[16,32,24]{2,1,0:T(8,128)(2,1)S(1)}, u32[]{:S(2)}, u32[]{:S(2)}) collective-permute-start(bf16[16,32,24]{2,1,0:T(8,128)(2,1)S(1)} %get-tuple-element.7), channel_id=1, source_target_pairs={{1,0},{3,2},{5,4},{7,6},{9,8},{11,10},{13,12},{15,14},{17,16},{19,... | collective-permute-start | bytes 73736 | tf_op jit(solution)/shard_map/ppermute | solution.py:23
  72.6 3.9 %copy-start.1 = (f32[32,16,1024]{2,0,1:T(8,128)S(1)}, f32[32,16,1024]{2,0,1:T(8,128)}, u32[]{:S(2)}) copy-start(f32[32,16,1024]{2,0,1:T(8,128)} %fusion.30) | copy-start | bytes 6291460
  72.6 3.9 %copy-start.2 = (f32[16,32,1024]{2,1,0:T(8,128)S(1)}, f32[16,32,1024]{2,1,0:T(8,128)}, u32[]{:S(2)}) copy-start(f32[16,32,1024]{2,1,0:T(8,128)} %reshape.196) | copy-start | bytes 6291460
  72.6 3.9 %copy-start.4 = (f32[16,1024]{1,0:T(8,128)S(1)}, f32[16,1024]{1,0:T(8,128)}, u32[]{:S(2)}) copy-start(f32[16,1024]{1,0:T(8,128)} %get-tuple-element.30) | copy-start | bytes 196612
  72.6 3.9 %copy-start.5 = (f32[16,1024]{1,0:T(8,128)S(1)}, f32[16,1024]{1,0:T(8,128)}, u32[]{:S(2)}) copy-start(f32[16,1024]{1,0:T(8,128)} %get-tuple-element.31) | copy-start | bytes 196612
where the time goes:
time: 95.9 us; the launch traced here: 95.5 us
  matrix products  25.4 us (26%)
  starting transfers between devices  18.6 us (19%)
  waiting for transfers between devices  14.2 us (15%)
  local copies, waits for them, and re-layouts  14.1 us (15%)
  blocking collectives  11.4 us (12%)
  other arithmetic  9.52 us (10%)
  between operations  2.24 us (2%)
    ppermute x3, starting transfers between devices, with_halo(): lax.ppermute(head, axis, [((i + 1) % count, i) for i in range(ends)])  15.3 us
    ppermute x3, waiting for transfers between devices, with_halo(): lax.ppermute(tail, axis, [(i, (i + 1) % count) for i in range(ends)])  13.1 us
    all_to_all x1, blocking collectives, local(): lax.all_to_all(detection, 'rd', split_axis=1, concat_axis=2, tiled=True)  11.4 us
    dot_general x2, matrix products, range_mean(): jnp.einsum('aqbs,sr->aqbr', value_blocks, banded, preferred_element_type=...  6.59 us
    convert_element_type x1, other arithmetic, local(): log_power = jnp.log(integrated + 0.05).astype(jnp.bfloat16)  5.83 us
    reshape x2, local copies, waits for them, and re-layouts, range_mean(): sums = sums.reshape(dwells, local_bins, local_cells)  4.41 us
    dot_general x1, matrix products, local(): jnp.einsum('asr,sk->akr', circled, doppler_lag_band, preferred_element_ty...  4.25 us
    dot_general x1, matrix products, local(): jnp.einsum('sb,sqr->bqr', lead_band, log_power, preferred_element_type=jn...  3.89 us
  transfers between devices with their start and end apart: 6, of which 3 were waited for; matrix products, arithmetic and copies ran while one was open for 21% of the time, Pallas kernels for 0%

commit v1 on v0

--- a/solution.py
+++ b/solution.py
@@ -147,7 +147,10 @@
     noise_level = jnp.maximum(noise_level, jnp.maximum(azimuth_lead, azimuth_lag))
     keep = weight[:, REACH_R : REACH_R + local_cells]
     detection = (keep[:, None, :] * (center.astype(jnp.float32) - noise_level)).astype(jnp.bfloat16)
-    detection = lax.all_to_all(detection, "rd", split_axis=1, concat_axis=2, tiled=True)
+    detection = jnp.concatenate(
+        lax.all_to_all(jnp.stack(jnp.split(detection, lax.axis_size("rd"), axis=1)), "rd", 0, 0),
+        axis=2,
+    )
     return detection
 
 

time: 95.9 us -> 94.2 us (0.982)
  local copies, waits for them, and re-layouts: 14.1 us -> 12 us
    all_to_all x2 -> x0, local copies, waits for them, and re-layouts: 2.68 us -> none  [local(): lax.all_to_all(detection, 'rd', split_axis=1, concat_axis=2, tiled=True)]
    reshape x0 -> x1, local copies, waits for them, and re-layouts: none -> 1.06 us  [local(): jnp.concatenate(lax.all_to_all(jnp.stack(jnp.split(detection, lax.axis_si...]
  transfers between devices with their start and end apart: 6 -> 6, of which waited for: 3 -> 3; matrix products, arithmetic and copies ran while one was open for 21% -> 22% of each run, Pallas kernels for 0% -> 0%
where the time goes in v1:
time: 94.2 us; the launch traced here: 93.8 us
  matrix products  25.7 us (27%)
  starting transfers between devices  18.6 us (20%)
  waiting for transfers between devices  14.1 us (15%)
  local copies, waits for them, and re-layouts  12 us (13%)
  blocking collectives  11.4 us (12%)
  other arithmetic  9.58 us (10%)
  between operations  2.29 us (2%)
    ppermute x3, starting transfers between devices, with_halo(): lax.ppermute(head, axis, [((i + 1) % count, i) for i in range(ends)])  15.3 us
    ppermute x3, waiting for transfers between devices, with_halo(): lax.ppermute(tail, axis, [(i, (i + 1) % count) for i in range(ends)])  13 us
    all_to_all x1, blocking collectives, local(): lax.all_to_all(jnp.stack(jnp.split(detection, lax.axis_size('rd'), axis=1...  11.4 us
    dot_general x2, matrix products, range_mean(): jnp.einsum('aqbs,sr->aqbr', value_blocks, banded, preferred_element_type=...  6.73 us
    convert_element_type x1, other arithmetic, local(): log_power = jnp.log(integrated + 0.05).astype(jnp.bfloat16)  5.79 us
    reshape x2, local copies, waits for them, and re-layouts, range_mean(): sums = sums.reshape(dwells, local_bins, local_cells)  4.4 us
    dot_general x1, matrix products, local(): jnp.einsum('asr,sk->akr', circled, doppler_lag_band, preferred_element_ty...  4.11 us
    dot_general x1, matrix products, local(): jnp.einsum('sb,sqr->bqr', lead_band, log_power, preferred_element_type=jn...  3.95 us
  transfers between devices with their start and end apart: 6, of which 3 were waited for; matrix products, arithmetic and copies ran while one was open for 22% of the time, Pallas kernels for 0%

profile of v1, /device:TPU:1, one launch (start us, length us, event | category | flops | bytes accessed | tf_op | source)
XLA Modules:
  0.0 93.8 jit_solution(8864147334610873267)
XLA Ops:
  0.0 0.7 fusion.75
  0.8 2.3 %convolution_bitcast_fusion = f32[2,16,32,1024]{3,2,1,0:T(8,128)S(1)} fusion(bf16[2,16,32,1024]{3,2,1,0:T(8,128)(2,1)} %param.5, bf16[1,32,2,32]{3,1,2,0:T(8,128)(2,1)S(1)} %get-tuple-element.16, bf16[1,32,2,32]{3,1,2,0:T(8,128)(2,1)S(1)} %get-tuple-element.15), kind=kOutput, calls=%fused_computation.11 | convolution fusion | flops 134234112 | bytes 6299648 | tf_op jit(solution)/shard_map/ckdp,dapr->cakr/dot_general | solution.py:56
  3.1 0.0 copy-start
  3.1 0.7 broadcast_multiply_fusion
  3.8 3.3 %collective-permute-start.1 = (f32[2,32,1024]{2,1,0:T(8,128)S(1)}, f32[2,32,1024]{2,1,0:T(8,128)S(1)}, u32[]{:S(2)}, u32[]{:S(2)}) collective-permute-start(f32[2,32,1024]{2,1,0:T(8,128)S(1)} %get-tuple-element.6), channel_id=1, source_target_pairs={{2,0},{4,2},{6,4},{8,6},{10,8},{12,10},{14,12},{16,14},{18,16},{20... | collective-permute-start | bytes 786440 | tf_op jit(solution)/shard_map/ppermute | solution.py:23
  7.1 0.0 copy-start.6
  7.1 0.0 copy-start.7
  7.1 0.0 copy-start.8
  7.1 1.0 %collective-permute-start = (f32[2,32,1024]{2,1,0:T(8,128)S(1)}, f32[2,32,1024]{2,1,0:T(8,128)S(1)}, u32[]{:S(2)}, u32[]{:S(2)}) collective-permute-start(f32[2,32,1024]{2,1,0:T(8,128)S(1)} %get-tuple-element.5), channel_id=1, source_target_pairs={{0,2},{2,4},{4,6},{6,8},{8,10},{10,12},{12,14},{14,16},{16,18},{18... | collective-permute-start | bytes 786440 | tf_op jit(solution)/shard_map/ppermute | solution.py:21
  8.1 0.0 copy-done
  8.2 0.5 fusion.129
  8.7 0.0 copy-done.6
  8.7 0.7 fusion.127
  9.3 0.0 copy-done.7
  9.3 0.7 fusion.126
  10.0 0.0 copy-done.8
  10.0 0.2 fusion.128
  10.3 1.0 %convolution_maximum_fusion = f32[16,8,128]{2,1,0:T(8,128)S(1)} fusion(f32[16,8,176]{2,0,1:T(8,128)S(1)} %constant_dynamic-update-slice_fusion, s32[]{:T(128)} %bitcast.27), kind=kOutput, calls=%fused_computation.45 | convolution fusion | flops 34732032 | bytes 155652 | tf_op jit(solution)/shard_map/abs,sr->abr/dot_general | solution.py:119
  11.2 1.0 %convolution_maximum_fusion.1 = f32[16,8,128]{2,1,0:T(8,128)S(1)} fusion(f32[16,8,176]{2,0,1:T(8,128)S(1)} %constant_dynamic-update-slice_fusion, s32[]{:T(128)} %bitcast.27, s32[128]{0:T(128)S(1)} %iota_add_fusion.3), kind=kOutput, calls=%fused_computation.46 | convolution fusion | flops 34709504 | bytes 156164 | tf_op jit(solution)/shard_map/abs,sr->abr/dot_general | solution.py:119
  12.2 0.1 slice.178
  14.2 0.7 copy_bitcast_fusion
  14.9 0.0 collective-permute-done.1
  14.9 1.8 %collective-permute-done = f32[2,32,1024]{2,1,0:T(8,128)S(1)} collective-permute-done((f32[2,32,1024]{2,1,0:T(8,128)S(1)}, f32[2,32,1024]{2,1,0:T(8,128)S(1)}, u32[]{:S(2)}, u32[]{:S(2)}) %collective-permute-start) | collective-permute-done | bytes 262176 | tf_op jit(solution)/shard_map/ppermute | solution.py:21
  16.6 0.0 copy-start.3
  16.6 0.7 copy-done.3
  17.3 5.8 %fusion.11 = bf16[16,32,1024]{2,1,0:T(8,128)(2,1)S(1)} fusion(f32[16,32,1024]{2,1,0:T(8,128)S(1)} %fusion.129, f32[2,32,1024]{2,1,0:T(8,128)S(1)} %collective-permute-done.1, f32[2,32,1024]{2,1,0:T(8,128)} %copy-done.3, f32[]{:T(128)} %bitcast.18, f32[]{:T(128)} %bitcast.16, f32[]{:T(128)} %bitcast.14, f32[]{:T(128)} %bitcast.13, f32[]{:T(128)} %bitcast.1, ...), kind=kLoop, calls=%fused_computation.18 | loop fusion | flops 9437184 | bytes 7864340 | tf_op jit(solution)/shard_map/convert_element_type | solution.py:64
  23.1 1.3 %fusion.125 = (bf16[12,32,1024]{2,1,0:T(8,128)(2,1)}, bf16[12,32,1024]{2,1,0:T(8,128)(2,1)}) fusion(bf16[16,32,1024]{2,1,0:T(8,128)(2,1)S(1)} %fusion.11), kind=kLoop, calls=%fused_computation.190 | loop fusion | bytes 3145728 | tf_op jit(solution)/shard_map/slice | solution.py:18
  24.5 0.1 fusion.124
  24.6 0.1 fusion.123
  24.7 10.6 %collective-permute-start.5 = (bf16[12,32,1024]{2,1,0:T(8,128)(2,1)}, bf16[12,32,1024]{2,1,0:T(8,128)(2,1)}, u32[]{:S(2)}, u32[]{:S(2)}) collective-permute-start(bf16[12,32,1024]{2,1,0:T(8,128)(2,1)} %get-tuple-element.14), channel_id=1, source_target_pairs={{2,0},{4,2},{6,4},{8,6},{10,8},{12,10},{14,12},{16,14},{18,16},{20... | collective-permute-start | bytes 2359304 | tf_op jit(solution)/shard_map/ppermute | solution.py:23
  35.3 0.0 collective-permute-start.4
  35.3 2.2 %collective-permute-start.2 = (bf16[16,32,24]{2,1,0:T(8,128)(2,1)S(1)}, bf16[16,32,24]{2,1,0:T(8,128)(2,1)S(1)}, u32[]{:S(2)}, u32[]{:S(2)}) collective-permute-start(bf16[16,32,24]{2,1,0:T(8,128)(2,1)S(1)} %get-tuple-element.10), channel_id=1, source_target_pairs={{0,1},{2,3},{4,5},{6,7},{8,9},{10,11},{12,13},{14,15},{16,17},{18,... | collective-permute-start | bytes 73736 | tf_op jit(solution)/shard_map/ppermute | solution.py:21
  37.5 1.5 %collective-permute-start.3 = (bf16[16,32,24]{2,1,0:T(8,128)(2,1)S(1)}, bf16[16,32,24]{2,1,0:T(8,128)(2,1)S(1)}, u32[]{:S(2)}, u32[]{:S(2)}) collective-permute-start(bf16[16,32,24]{2,1,0:T(8,128)(2,1)S(1)} %get-tuple-element.9), channel_id=1, source_target_pairs={{1,0},{3,2},{5,4},{7,6},{9,8},{11,10},{13,12},{15,14},{17,16},{19,... | collective-permute-start | bytes 73736 | tf_op jit(solution)/shard_map/ppermute | solution.py:23
  39.0 2.7 %fusion.30 = f32[32,16,1024]{2,0,1:T(8,128)} fusion(bf16[16,4,1024]{2,1,0:T(4,128)(2,1)S(1)} %get-tuple-element.12, bf16[16,32,1024]{2,1,0:T(8,128)(2,1)S(1)} %fusion.11, bf16[16,4,1024]{2,1,0:T(4,128)(2,1)S(1)} %get-tuple-element.11, s32[]{:T(128)} %bitcast.42, s32[32]{0:T(128)S(1)} %iota_add_fusion.2), kind=kOutput, calls=%fused_computation.47 | convolution fusion | flops 45880320 | bytes 3408004 | tf_op jit(solution)/shard_map/asr,sk->akr/dot_general | solution.py:137
  41.7 11.2 %collective-permute-done.2 = bf16[16,32,24]{2,1,0:T(8,128)(2,1)S(1)} collective-permute-done((bf16[16,32,24]{2,1,0:T(8,128)(2,1)S(1)}, bf16[16,32,24]{2,1,0:T(8,128)(2,1)S(1)}, u32[]{:S(2)}, u32[]{:S(2)}) %collective-permute-start.2) | collective-permute-done | bytes 24608 | tf_op jit(solution)/shard_map/ppermute | solution.py:21
  52.9 1.1 %collective-permute-done.3 = bf16[16,32,24]{2,1,0:T(8,128)(2,1)S(1)} collective-permute-done((bf16[16,32,24]{2,1,0:T(8,128)(2,1)S(1)}, bf16[16,32,24]{2,1,0:T(8,128)(2,1)S(1)}, u32[]{:S(2)}, u32[]{:S(2)}) %collective-permute-start.3) | collective-permute-done | bytes 24608 | tf_op jit(solution)/shard_map/ppermute | solution.py:23
  54.0 1.9 %concatenate.20 = bf16[16,32,1072]{2,1,0:T(8,128)(2,1)S(1)} concatenate(bf16[16,32,24]{2,1,0:T(8,128)(2,1)S(1)} %collective-permute-done.2, bf16[16,32,1024]{2,1,0:T(8,128)(2,1)S(1)} %fusion.11, bf16[16,32,24]{2,1,0:T(8,128)(2,1)S(1)} %collective-permute-done.3), dimensions={2} | concatenate | bytes 2195456 | tf_op jit(solution)/shard_map/concatenate | solution.py:19
  56.0 0.1 broadcast_multiply_fusion.1
  56.3 3.4 %fusion.26 = f32[16,32,8,128]{3,2,1,0:T(8,128)} fusion(bf16[16,32,8,176]{3,1,0,2:T(8,128)(2,1)S(1)} %fusion.31, s32[]{:T(128)} %bitcast.27), kind=kOutput, calls=%fused_computation.40 | convolution fusion | flops 184662016 | bytes 3538948 | tf_op jit(solution)/shard_map/aqbs,sr->aqbr/dot_general | solution.py:117
  59.7 2.7 %reshape.202 = f32[16,32,1024]{2,1,0:T(8,128)} reshape(f32[16,32,8,128]{3,2,1,0:T(8,128)} %fusion.26) | data formatting | bytes 4194304 | tf_op jit(solution)/shard_map/reshape | solution.py:118
  62.4 3.4 %fusion.28 = f32[16,32,8,128]{3,2,1,0:T(8,128)} fusion(bf16[16,32,8,176]{3,1,0,2:T(8,128)(2,1)S(1)} %fusion.31, s32[]{:T(128)} %bitcast.27, s32[128]{0:T(128)S(1)} %iota_add_fusion.3), kind=kOutput, calls=%fused_computation.42 | convolution fusion | flops 184639488 | bytes 3539460 | tf_op jit(solution)/shard_map/aqbs,sr->aqbr/dot_general | solution.py:117
  65.8 1.7 %reshape.201 = f32[16,32,1024]{2,1,0:T(8,128)S(1)} reshape(f32[16,32,8,128]{3,2,1,0:T(8,128)} %fusion.28) | data formatting | bytes 4194304 | tf_op jit(solution)/shard_map/reshape | solution.py:118
  67.5 0.0 collective-permute-done.5
  67.5 0.0 collective-permute-done.4
  67.5 1.7 %pad_maximum_fusion = bf16[40,32,1024]{2,1,0:T(8,128)(2,1)S(1)} fusion(bf16[12,32,1024]{2,1,0:T(8,128)(2,1)} %collective-permute-done.5, bf16[16,32,1024]{2,1,0:T(8,128)(2,1)S(1)} %fusion.11, bf16[12,32,1024]{2,1,0:T(8,128)(2,1)} %collective-permute-done.4), kind=kLoop, calls=%fused_computation | loop fusion | flops 2621440 | bytes 5242880 | tf_op jit(solution)/shard_map/concatenate | solution.py:19
  69.2 3.8 %fusion = f32[16,32,1024]{2,0,1:T(8,128)S(1)} fusion(bf16[40,32,1024]{2,1,0:T(8,128)(2,1)S(1)} %pad_maximum_fusion, s32[]{:T(128)} %bitcast.47), kind=kOutput, calls=%fused_computation.5 | convolution fusion | flops 41946240 | bytes 4718596 | tf_op jit(solution)/shard_map/sb,sqr->bqr/dot_general | solution.py:80
  73.0 0.0 copy-start.1
  73.0 0.0 copy-start.2
  73.0 0.0 copy-start.4
  73.0 0.0 copy-start.5
  73.0 3.9 %fusion.2 = f32[16,32,1024]{2,0,1:T(8,128)S(1)} fusion(bf16[40,32,1024]{2,1,0:T(8,128)(2,1)S(1)} %pad_maximum_fusion, s32[]{:T(128)} %bitcast.47, s32[16]{0:T(128)S(1)} %iota_add_fusion.1), kind=kOutput, calls=%fused_computation.7 | convolution fusion | flops 41945600 | bytes 4718660 | tf_op jit(solution)/shard_map/sb,sqr->bqr/dot_general | solution.py:76
  76.9 0.0 copy-done.1
  76.9 0.0 copy-done.2
  76.9 0.0 copy-done.4
  76.9 0.0 copy-done.5
  77.0 4.1 %fusion.22 = bf16[16,32,1024]{2,1,0:T(8,128)(2,1)S(1)} fusion(f32[16,32,1024]{2,0,1:T(8,128)S(1)} %fusion, f32[16,32,1024]{2,0,1:T(8,128)S(1)} %fusion.2, f32[32,16,1024]{2,0,1:T(8,128)S(1)} %copy-done.1, f32[16,32,1024]{2,1,0:T(8,128)S(1)} %copy-done.2, f32[16,32,1024]{2,1,0:T(8,128)S(1)} %reshape.201, bf16[16,32,1024]{2,1,0:T(8,128)(2,1)S(1)} %fusion.11, ...), kind=kOutput, calls=%fused_computation.34 | convolution fusion | flops 53745920 | bytes 13041676 | tf_op jit(solution)/shard_map/asr,sk->akr/dot_general | solution.py:141
  81.1 0.1 slice_bitcast_fusion.1
  81.2 0.1 pad_maximum_fusion.6
  81.3 11.4 %all_to_all.5 = bf16[2,16,16,1024]{3,2,1,0:T(8,128)(2,1)S(1)} all-to-all(bf16[2,16,16,1024]{3,2,1,0:T(8,128)(2,1)S(1)} %pad_maximum_fusion.6), channel_id=1, replica_groups=mesh['az'=128,'rd'=2] {'rd'}, dimensions={0} | all-to-all | bytes 2097152 | tf_op jit(solution)/shard_map/all_to_all | solution.py:151
  92.7 1.1 %copy.29 = bf16[2,16,2,8,1024]{4,3,0,2,1:T(8,128)(2,1)} copy(bf16[2,16,2,8,1024]{4,3,2,1,0:T(8,128)(2,1)S(1)} %bitcast.156) | data formatting | bytes 2097152 | tf_op jit(solution)/shard_map/reshape | solution.py:150
  (23 shorter events, 0.3 us)
Async XLA Ops:
  3.1 5.0 %copy-start = (f32[2,16,32,1024]{3,2,1,0:T(8,128)}, f32[2,16,32,1024]{3,2,1,0:T(8,128)S(1)}, u32[]{:S(2)}) copy-start(f32[2,16,32,1024]{3,2,1,0:T(8,128)S(1)} %convolution_bitcast_fusion) | copy-start | bytes 12582916
  3.8 11.0 %collective-permute-start.1 = (f32[2,32,1024]{2,1,0:T(8,128)S(1)}, f32[2,32,1024]{2,1,0:T(8,128)S(1)}, u32[]{:S(2)}, u32[]{:S(2)}) collective-permute-start(f32[2,32,1024]{2,1,0:T(8,128)S(1)} %get-tuple-element.6), channel_id=1, source_target_pairs={{2,0},{4,2},{6,4},{8,6},{10,8},{12,10},{14,12},{16,14},{18,16},{20... | collective-permute-start | bytes 786440 | tf_op jit(solution)/shard_map/ppermute | solution.py:23
  7.1 1.6 %copy-start.6 = (f32[5]{0:T(128)S(1)}, f32[5]{0:T(128)}, u32[]{:S(2)}) copy-start(f32[5]{0:T(128)} %param.7) | copy-start | bytes 64
  7.1 2.2 %copy-start.7 = (s32[6]{0:T(128)S(1)}, s32[6]{0:T(128)}, u32[]{:S(2)}) copy-start(s32[6]{0:T(128)} %param.9) | copy-start | bytes 76
  7.1 2.9 %copy-start.8 = (s32[16,16]{1,0:T(8,128)S(1)}, s32[16,16]{1,0:T(8,128)}, u32[]{:S(2)}) copy-start(s32[16,16]{1,0:T(8,128)} %param.8) | copy-start | bytes 3076
  7.1 9.5 %collective-permute-start = (f32[2,32,1024]{2,1,0:T(8,128)S(1)}, f32[2,32,1024]{2,1,0:T(8,128)S(1)}, u32[]{:S(2)}, u32[]{:S(2)}) collective-permute-start(f32[2,32,1024]{2,1,0:T(8,128)S(1)} %get-tuple-element.5), channel_id=1, source_target_pairs={{0,2},{2,4},{4,6},{6,8},{8,10},{10,12},{12,14},{14,16},{16,18},{18... | collective-permute-start | bytes 786440 | tf_op jit(solution)/shard_map/ppermute | solution.py:21
  16.6 0.7 copy-start.3
  24.7 42.8 %collective-permute-start.5 = (bf16[12,32,1024]{2,1,0:T(8,128)(2,1)}, bf16[12,32,1024]{2,1,0:T(8,128)(2,1)}, u32[]{:S(2)}, u32[]{:S(2)}) collective-permute-start(bf16[12,32,1024]{2,1,0:T(8,128)(2,1)} %get-tuple-element.14), channel_id=1, source_target_pairs={{2,0},{4,2},{6,4},{8,6},{10,8},{12,10},{14,12},{16,14},{18,16},{20... | collective-permute-start | bytes 2359304 | tf_op jit(solution)/shard_map/ppermute | solution.py:23
  35.3 32.2 %collective-permute-start.4 = (bf16[12,32,1024]{2,1,0:T(8,128)(2,1)}, bf16[12,32,1024]{2,1,0:T(8,128)(2,1)}, u32[]{:S(2)}, u32[]{:S(2)}) collective-permute-start(bf16[12,32,1024]{2,1,0:T(8,128)(2,1)} %get-tuple-element.13), channel_id=1, source_target_pairs={{0,2},{2,4},{4,6},{6,8},{8,10},{10,12},{12,14},{14,16},{16,18},{18... | collective-permute-start | bytes 2359304 | tf_op jit(solution)/shard_map/ppermute | solution.py:21
  35.3 17.6 %collective-permute-start.2 = (bf16[16,32,24]{2,1,0:T(8,128)(2,1)S(1)}, bf16[16,32,24]{2,1,0:T(8,128)(2,1)S(1)}, u32[]{:S(2)}, u32[]{:S(2)}) collective-permute-start(bf16[16,32,24]{2,1,0:T(8,128)(2,1)S(1)} %get-tuple-element.10), channel_id=1, source_target_pairs={{0,1},{2,3},{4,5},{6,7},{8,9},{10,11},{12,13},{14,15},{16,17},{18,... | collective-permute-start | bytes 73736 | tf_op jit(solution)/shard_map/ppermute | solution.py:21
  37.5 16.5 %collective-permute-start.3 = (bf16[16,32,24]{2,1,0:T(8,128)(2,1)S(1)}, bf16[16,32,24]{2,1,0:T(8,128)(2,1)S(1)}, u32[]{:S(2)}, u32[]{:S(2)}) collective-permute-start(bf16[16,32,24]{2,1,0:T(8,128)(2,1)S(1)} %get-tuple-element.9), channel_id=1, source_target_pairs={{1,0},{3,2},{5,4},{7,6},{9,8},{11,10},{13,12},{15,14},{17,16},{19,... | collective-permute-start | bytes 73736 | tf_op jit(solution)/shard_map/ppermute | solution.py:23
  73.0 4.0 %copy-start.1 = (f32[32,16,1024]{2,0,1:T(8,128)S(1)}, f32[32,16,1024]{2,0,1:T(8,128)}, u32[]{:S(2)}) copy-start(f32[32,16,1024]{2,0,1:T(8,128)} %fusion.30) | copy-start | bytes 6291460
  73.0 4.0 %copy-start.2 = (f32[16,32,1024]{2,1,0:T(8,128)S(1)}, f32[16,32,1024]{2,1,0:T(8,128)}, u32[]{:S(2)}) copy-start(f32[16,32,1024]{2,1,0:T(8,128)} %reshape.202) | copy-start | bytes 6291460
  73.0 4.0 %copy-start.4 = (f32[16,1024]{1,0:T(8,128)S(1)}, f32[16,1024]{1,0:T(8,128)}, u32[]{:S(2)}) copy-start(f32[16,1024]{1,0:T(8,128)} %get-tuple-element.32) | copy-start | bytes 196612
  73.0 4.0 %copy-start.5 = (f32[16,1024]{1,0:T(8,128)S(1)}, f32[16,1024]{1,0:T(8,128)}, u32[]{:S(2)}) copy-start(f32[16,1024]{1,0:T(8,128)} %get-tuple-element.33) | copy-start | bytes 196612
